TPU v7x, 32 devices: a whole 2x2x4 slice. The times are simulated.
32 devices in a mesh: dp: 8 (over z, y), tensor: 4 (over x, core).
Axes of the slice: x: 2, y: 2, z: 4, core: 2. Of those that a mesh axis runs over, the one named last changes fastest.
Arguments:
- inputs: bfloat16 [608, 8, 1024], P('tensor', 'dp'), may hold values from -6 to 6
- attn_gain: bfloat16 [2, 1024], P(None, 'dp'), may hold values from 0.5 to 1.5
- attn_shift: bfloat16 [2, 1024], P(None, 'dp'), may hold values from -1.25 to 1.25
- qkv_weight: bfloat16 [2, 1024, 3, 1024], P(None, 'dp', None, 'tensor'), may hold values from -0.1875 to 0.1875
- query_bias: bfloat16 [2, 1024], P(None, 'dp'), may hold values from -3 to 3
- value_bias: bfloat16 [2, 1024], P(None, 'dp'), may hold values from -1.25 to 1.25
- out_weight: bfloat16 [2, 1024, 1024], P(None, 'tensor', 'dp'), may hold values from -2 to 2
- out_bias: bfloat16 [2, 1024], P(None, 'dp'), may hold values from -1.25 to 1.25
- mlp_gain: bfloat16 [2, 1024], P(None, 'dp'), may hold values from 0.5 to 1.5
- mlp_shift: bfloat16 [2, 1024], P(None, 'dp'), may hold values from -1.25 to 1.25
- up_weight: bfloat16 [2, 1024, 4096], P(None, 'dp', 'tensor'), may hold values from -0.1875 to 0.1875
- up_bias: bfloat16 [2, 4096], P(None, 'dp'), may hold values from -1.25 to 1.25
- down_weight: bfloat16 [2, 4096, 1024], P(None, 'tensor', 'dp'), may hold values from -0.09375 to 0.09375
- down_bias: bfloat16 [2, 1024], P(None, 'dp'), may hold values from -1.25 to 1.25
- cotangent: bfloat16 [608, 8, 1024], P('tensor', 'dp'), may hold values from -6 to 6
- image_mask: int32 [8], P('dp'), may hold values 0 or 1
- row_mask: int32 [608, 8], P(None, 'dp'), may hold values from 0 to 1, as said below
Outputs:
- outputs: bfloat16 [608, 8, 1024], P('tensor', 'dp')
- grad_inputs: float32 [608, 8, 1024], P('tensor', 'dp')
- grad_attn_gain: float32 [2, 1024], P(None, 'dp')
- grad_attn_shift: float32 [2, 1024], P(None, 'dp')
- grad_qkv_weight: float32 [2, 1024, 3, 1024], P(None, 'dp', None, 'tensor')
- grad_query_bias: float32 [2, 1024], P(None, 'dp')
- grad_value_bias: float32 [2, 1024], P(None, 'dp')
- grad_out_weight: float32 [2, 1024, 1024], P(None, 'tensor', 'dp')
- grad_out_bias: float32 [2, 1024], P(None, 'dp')
- grad_mlp_gain: float32 [2, 1024], P(None, 'dp')
- grad_mlp_shift: float32 [2, 1024], P(None, 'dp')
- grad_up_weight: float32 [2, 1024, 4096], P(None, 'dp', 'tensor')
- grad_up_bias: float32 [2, 4096], P(None, 'dp')
- grad_down_weight: float32 [2, 4096, 1024], P(None, 'tensor', 'dp')
- grad_down_bias: float32 [2, 1024], P(None, 'dp')
Inputs may be any that keep to these rules, and one draw needn't show every extreme that they name: `row_mask`: row 0 of every image is live; rows 577 and later are 0.
All inputs are finite; a program needn't handle non-finite values. No bound on the sum of `image_mask` on one device may be relied on, other than what follows from the above.
Results may differ from a plain program's by a relative error of at most 0.015.
Values may be sent and summed in bfloat16 or wider, within the bound.
A program may use at most 128 MiB of HBM per device.

v0:
```python
import jax
import jax.numpy as jnp
from jax import lax
from jax.sharding import PartitionSpec as P

HEAD_DIM = 64


def layer_norm(values, gain, shift):
    center = values - jnp.mean(values, -1, keepdims=True)
    inverse = lax.rsqrt(jnp.mean(center * center, -1, keepdims=True) + 1e-05)
    return center * inverse * gain + shift


def norm_backward(values, gain, grad_out):
    center = values - jnp.mean(values, -1, keepdims=True)
    inverse = lax.rsqrt(jnp.mean(center * center, -1, keepdims=True) + 1e-05)
    normal = center * inverse
    grad_hat = grad_out * gain
    grad_in = inverse * (
        grad_hat
        - jnp.mean(grad_hat, -1, keepdims=True)
        - normal * jnp.mean(grad_hat * normal, -1, keepdims=True)
    )
    return (grad_in, jnp.sum(grad_out * normal, (0, 1)), jnp.sum(grad_out, (0, 1)))


def quick_gelu(values):
    return values * jax.nn.sigmoid(1.702 * values)


def gelu_slope(values):
    sigma = jax.nn.sigmoid(1.702 * values)
    return sigma + 1.702 * values * sigma * (1.0 - sigma)


def image_scores(block, keep):
    scores = jnp.einsum(
        "qhe,khe->hqk", block[:, 0], block[:, 1], preferred_element_type=jnp.float32
    )
    scores = scores * HEAD_DIM ** (-0.5)
    return jnp.where(keep[None, None, :], scores, -1e30)


def attention_forward(qkv, row_mask):
    seq_len, images, width = (qkv.shape[0], qkv.shape[1], qkv.shape[3])
    heads = width // HEAD_DIM

    def one_image(which, carry):
        outs, lses = carry
        block = lax.dynamic_index_in_dim(qkv, which, 1, keepdims=False).reshape(
            seq_len, 3, heads, HEAD_DIM
        )
        keep = lax.dynamic_index_in_dim(row_mask, which, 1, keepdims=False) > 0
        scores = image_scores(block, keep)
        row_max = jnp.max(scores, -1, keepdims=True)
        expo = jnp.exp(scores - row_max)
        row_total = jnp.sum(expo, -1, keepdims=True)
        weights = (expo / row_total).astype(jnp.bfloat16)
        values = jnp.einsum(
            "hqk,khe->qhe", weights, block[:, 2], preferred_element_type=jnp.float32
        )
        values = values.astype(jnp.bfloat16).reshape(seq_len, 1, width)
        outs = values
        lses = lax.dynamic_update_index_in_dim(
            lses, (row_max + jnp.log(row_total))[:, :, 0], which, 0
        )
        return (outs, lses)

    start = (
        jnp.zeros((seq_len, images, width), jnp.bfloat16),
        jnp.zeros((images, heads, seq_len), jnp.float32),
    )
    return lax.fori_loop(0, images, one_image, start)


def attention_backward(qkv, lses, grad_mixed, row_mask):
    seq_len, images, width = (qkv.shape[0], qkv.shape[1], qkv.shape[3])
    heads = width // HEAD_DIM
    scale = HEAD_DIM ** (-0.5)

    def one_image(which, grads):
        block = lax.dynamic_index_in_dim(qkv, which, 1, keepdims=False).reshape(
            seq_len, 3, heads, HEAD_DIM
        )
        keep = lax.dynamic_index_in_dim(row_mask, which, 1, keepdims=False) > 0
        grad_out = lax.dynamic_index_in_dim(grad_mixed, which, 1, keepdims=False).reshape(
            seq_len, heads, HEAD_DIM
        )
        lse_here = lax.dynamic_index_in_dim(lses, which, 0, keepdims=False)
        weights = jnp.exp(image_scores(block, keep) - lse_here[:, :, None])
        grad_value = jnp.einsum(
            "hqk,qhe->khe",
            weights.astype(jnp.bfloat16),
            grad_out,
            preferred_element_type=jnp.float32,
        )
        grad_weights = jnp.einsum(
            "qhe,khe->hqk", grad_out, block[:, 2], preferred_element_type=jnp.float32
        )
        delta = jnp.sum(weights * grad_weights, -1, keepdims=True)
        grad_scores = (weights * (grad_weights - delta)).astype(jnp.bfloat16)
        grad_query = (
            jnp.einsum("hqk,khe->qhe", grad_scores, block[:, 1], preferred_element_type=jnp.float32)
            * scale
        )
        grad_key = (
            jnp.einsum("hqk,qhe->khe", grad_scores, block[:, 0], preferred_element_type=jnp.float32)
            * scale
        )
        stacked = jnp.stack([grad_query, grad_key, grad_value], 1).astype(jnp.bfloat16)
        return stacked.reshape(seq_len, 1, 3, width)

    return lax.fori_loop(0, images, one_image, jnp.zeros(qkv.shape, jnp.bfloat16))


def body(
    inputs,
    attn_gain,
    attn_shift,
    qkv_weight,
    query_bias,
    value_bias,
    out_weight,
    out_bias,
    mlp_gain,
    mlp_shift,
    up_weight,
    up_bias,
    down_weight,
    down_bias,
    cotangent,
    image_mask,
    row_mask,
):
    depth_count = qkv_weight.shape[0]
    tensor_rank = lax.axis_index("tensor")
    local_rows = inputs.shape[0]
    head_width = qkv_weight.shape[3]
    unit_width = up_weight.shape[2]
    vectors = jnp.stack(
        [attn_gain, attn_shift, query_bias, value_bias, out_bias, mlp_gain, mlp_shift, down_bias], 1
    )

    def fetch(depth):
        return (
            lax.all_gather(qkv_weight[depth], "dp", axis=0, tiled=True),
            lax.all_gather(up_weight[depth], "dp", axis=0, tiled=True),
            lax.all_gather(out_weight[depth], "dp", axis=1, tiled=True),
            lax.all_gather(down_weight[depth], "dp", axis=1, tiled=True),
            lax.all_gather(vectors[depth], "dp", axis=1, tiled=True),
            lax.all_gather(up_bias[depth], "dp", axis=0, tiled=True),
        )

    def unpack(weights):
        vec = weights[4].astype(jnp.float32)
        query_cols = lax.dynamic_slice_in_dim(vec[2], tensor_rank * head_width, head_width)
        value_cols = lax.dynamic_slice_in_dim(vec[3], tensor_rank * head_width, head_width)
        bias_three = jnp.stack([query_cols, jnp.zeros_like(query_cols), value_cols])
        up_cols = lax.dynamic_slice_in_dim(
            weights[5].astype(jnp.float32), tensor_rank * unit_width, unit_width
        )
        return (vec, bias_three, up_cols)

    def forward_parts(hidden, weights):
        qkv_w, up_w, out_w = (weights[0], weights[1], weights[2])
        vec, bias_three, up_cols = unpack(weights)
        normed = layer_norm(hidden, vec[0], vec[1]).astype(jnp.bfloat16)
        product = jnp.einsum(
            "sid,dce->sice",
            lax.all_gather(normed, "tensor", axis=0, tiled=True),
            qkv_w,
            preferred_element_type=jnp.float32,
        )
        qkv = (product + bias_three).astype(jnp.bfloat16)
        mixed, lses = attention_forward(qkv, row_mask)
        middle = (
            hidden
            + lax.psum_scatter(
                jnp.einsum("sie,ed->sid", mixed, out_w, preferred_element_type=jnp.float32).astype(
                    jnp.bfloat16
                ),
                "tensor",
                scatter_dimension=0,
                tiled=True,
            ).astype(jnp.float32)
            + vec[4]
        )
        normed_mid = layer_norm(middle, vec[5], vec[6]).astype(jnp.bfloat16)
        before = (
            jnp.einsum(
                "sid,df->sif",
                lax.all_gather(normed_mid, "tensor", axis=0, tiled=True),
                up_w,
                preferred_element_type=jnp.float32,
            )
            + up_cols
        )
        active = quick_gelu(before).astype(jnp.bfloat16)
        return (normed, qkv, mixed, lses, middle, normed_mid, before, active)

    hidden = inputs.astype(jnp.float32)
    kept = []
    layer_inputs = []
    stored = []
    for depth in range(depth_count):
        weights = fetch(depth)
        kept.append(weights)
        layer_inputs.append(hidden)
        parts = forward_parts(hidden, weights)
        stored.append(parts)
        down_cols = weights[4][7].astype(jnp.float32)
        mlp_active = parts[7]
        mlp_down_w = weights[3]
        hidden = (
            parts[4]
            + lax.psum_scatter(
                jnp.einsum(
                    "sif,fd->sid", mlp_active, mlp_down_w, preferred_element_type=jnp.float32
                ).astype(jnp.bfloat16),
                "tensor",
                scatter_dimension=0,
                tiled=True,
            ).astype(jnp.float32)
            + down_cols
        )
    live_rows = lax.dynamic_slice_in_dim(row_mask, tensor_rank * local_rows, local_rows, 0)
    live = (live_rows * image_mask[None, :]).astype(jnp.float32)
    grad = cotangent.astype(jnp.float32) * live[:, :, None]
    per_layer = []
    for depth in reversed(range(depth_count)):
        weights = fetch(depth)
        parts = forward_parts(layer_inputs[depth], weights)
        layer_qkv_w = weights[0]
        layer_up_w = weights[1]
        layer_out_w = weights[2]
        down_w = weights[3]
        layer_vec, layer_bias_three, layer_up_cols = unpack(weights)
        (
            layer_normed,
            layer_qkv,
            layer_mixed,
            layer_lses,
            layer_middle,
            layer_normed_mid,
            layer_before,
            layer_active,
        ) = parts
        full_width = layer_vec.shape[1]
        grad_down_bias = jnp.sum(grad, (0, 1))
        fold_piece = lax.all_gather(grad.astype(jnp.bfloat16), "tensor", axis=0, tiled=True)
        update = jnp.einsum("sid,fd->sif", fold_piece, down_w, preferred_element_type=jnp.float32)
        grad_down_w = jnp.einsum(
            "sif,sid->fd", layer_active, fold_piece, preferred_element_type=jnp.float32
        )
        grad_before = (update * gelu_slope(layer_before)).astype(jnp.bfloat16)
        grad_up_cols = jnp.sum(grad_before.astype(jnp.float32), (0, 1))
        grad_up_w = jnp.einsum(
            "sid,sif->df",
            lax.all_gather(layer_normed_mid, "tensor", axis=0, tiled=True),
            grad_before,
            preferred_element_type=jnp.float32,
        )
        grad_normed_mid = lax.psum_scatter(
            jnp.einsum(
                "sif,df->sid", grad_before, layer_up_w, preferred_element_type=jnp.float32
            ).astype(jnp.bfloat16),
            "tensor",
            scatter_dimension=0,
            tiled=True,
        ).astype(jnp.float32)
        grad_mid, grad_mlp_gain, grad_mlp_shift = norm_backward(
            layer_middle, layer_vec[5], grad_normed_mid
        )
        grad_mid = grad_mid + grad
        grad_out_bias = jnp.sum(grad_mid, (0, 1))
        piece = lax.all_gather(grad_mid.astype(jnp.bfloat16), "tensor", axis=0, tiled=True)
        fold_update = jnp.einsum(
            "sid,ed->sie", piece, layer_out_w, preferred_element_type=jnp.float32
        )
        grad_out_w = jnp.einsum(
            "sie,sid->ed", layer_mixed, piece, preferred_element_type=jnp.float32
        )
        grad_qkv = attention_backward(
            layer_qkv, layer_lses, fold_update.astype(jnp.bfloat16), row_mask
        )
        grad_bias_three = jnp.sum(grad_qkv.astype(jnp.float32), (0, 1))
        grad_qkv_w = jnp.einsum(
            "sid,sice->dce",
            lax.all_gather(layer_normed, "tensor", axis=0, tiled=True),
            grad_qkv,
            preferred_element_type=jnp.float32,
        )
        grad_normed = lax.psum_scatter(
            jnp.einsum(
                "sice,dce->sid", grad_qkv, layer_qkv_w, preferred_element_type=jnp.float32
            ).astype(jnp.bfloat16),
            "tensor",
            scatter_dimension=0,
            tiled=True,
        ).astype(jnp.float32)
        grad_in, grad_attn_gain, grad_attn_shift = norm_backward(
            layer_inputs[depth], layer_vec[0], grad_normed
        )
        grad_in = grad_in + grad_mid
        empty = jnp.zeros((full_width,), jnp.float32)
        grad_query = lax.dynamic_update_slice_in_dim(
            empty, grad_bias_three[0], tensor_rank * head_width, 0
        )
        grad_value = lax.dynamic_update_slice_in_dim(
            empty, grad_bias_three[2], tensor_rank * head_width, 0
        )
        grad_up_full = lax.dynamic_update_slice_in_dim(
            jnp.zeros((weights[5].shape[0],), jnp.float32),
            grad_up_cols,
            tensor_rank * unit_width,
            0,
        )
        grad_vec = jnp.stack(
            [
                grad_attn_gain,
                grad_attn_shift,
                grad_query,
                grad_value,
                grad_out_bias,
                grad_mlp_gain,
                grad_mlp_shift,
                grad_down_bias,
            ]
        )
        shards = (
            lax.psum_scatter(grad_qkv_w, "dp", scatter_dimension=0, tiled=True),
            lax.psum_scatter(grad_up_w, "dp", scatter_dimension=0, tiled=True),
            lax.psum_scatter(grad_out_w, "dp", scatter_dimension=1, tiled=True),
            lax.psum_scatter(grad_down_w, "dp", scatter_dimension=1, tiled=True),
            lax.psum_scatter(grad_vec, "dp", scatter_dimension=1, tiled=True),
            lax.psum_scatter(grad_up_full, "dp", scatter_dimension=0, tiled=True),
        )
        grad, shards = (grad_in, shards)
        per_layer.insert(0, shards)
    vec_grads = jnp.stack([shards[4] for shards in per_layer])
    bias_grads = jnp.stack([shards[5] for shards in per_layer])
    vec_sum, up_sum = lax.psum((vec_grads, bias_grads), "tensor")
    return (
        hidden.astype(jnp.bfloat16),
        grad,
        vec_sum[:, 0],
        vec_sum[:, 1],
        jnp.stack([shards[0] for shards in per_layer]),
        vec_sum[:, 2],
        vec_sum[:, 3],
        jnp.stack([shards[2] for shards in per_layer]),
        vec_sum[:, 4],
        vec_sum[:, 5],
        vec_sum[:, 6],
        jnp.stack([shards[1] for shards in per_layer]),
        up_sum,
        jnp.stack([shards[3] for shards in per_layer]),
        vec_sum[:, 7],
    )


def solution(mesh):
    in_specs = (
        P("tensor", "dp", None),
        P(None, "dp"),
        P(None, "dp"),
        P(None, "dp", None, "tensor"),
        P(None, "dp"),
        P(None, "dp"),
        P(None, "tensor", "dp"),
        P(None, "dp"),
        P(None, "dp"),
        P(None, "dp"),
        P(None, "dp", "tensor"),
        P(None, "dp"),
        P(None, "tensor", "dp"),
        P(None, "dp"),
        P("tensor", "dp", None),
        P("dp"),
        P(None, "dp"),
    )
    out_specs = (
        P("tensor", "dp", None),
        P("tensor", "dp", None),
        P(None, "dp"),
        P(None, "dp"),
        P(None, "dp", None, "tensor"),
        P(None, "dp"),
        P(None, "dp"),
        P(None, "tensor", "dp"),
        P(None, "dp"),
        P(None, "dp"),
        P(None, "dp"),
        P(None, "dp", "tensor"),
        P(None, "dp"),
        P(None, "tensor", "dp"),
        P(None, "dp"),
    )
    return jax.shard_map(body, mesh=mesh, in_specs=in_specs, out_specs=out_specs, check_vma=False)
```

profile of v0, /device:TPU:0, one launch (start us, length us, event | category | flops | bytes accessed | tf_op | source)
XLA Modules:
  0.0 1577.7 jit_solution(11736033393084943452)
XLA Ops:
  14.9 22.4 %all-gather = bf16[1,8,1024]{2,0,1:T(2,128)(2,1)S(1)} all-gather(bf16[1,8,128]{2,0,1:T(2,128)(2,1)S(1)} %get-tuple-element.224), channel_id=2, replica_groups=mesh['dp'=8,'tensor'=4] {'dp'}, dimensions={2}, use_global_device_ids=true | all-gather | bytes 18432 | tf_op jit(solution)/shard_map/all_gather | solution.py:151
  41.3 16.5 %all-gather.6 = bf16[1,8,1024]{2,0,1:T(2,128)(2,1)S(1)} all-gather(bf16[1,8,128]{2,0,1:T(2,128)(2,1)S(1)} %get-tuple-element.225), channel_id=8, replica_groups=mesh['dp'=8,'tensor'=4] {'dp'}, dimensions={2}, use_global_device_ids=true | all-gather | bytes 18432 | tf_op jit(solution)/shard_map/all_gather | solution.py:151
  58.0 28.1 %all-gather.2 = bf16[1,256,1024]{2,1,0:T(8,128)(2,1)S(1)} all-gather(bf16[1,256,128]{2,1,0:T(8,128)(2,1)S(1)} %get-tuple-element.201), channel_id=4, replica_groups=mesh['dp'=8,'tensor'=4] {'dp'}, dimensions={2}, use_global_device_ids=true | all-gather | bytes 589824 | tf_op jit(solution)/shard_map/all_gather | solution.py:149
  86.2 16.8 %all-gather.43.cloned.1.call-done = bf16[1,1024,3,256]{3,1,2,0:T(8,128)(2,1)} async-done(((bf16[1,128,3,256]{3,1,2,0:T(8,128)(2,1)}), bf16[1,1024,3,256]{3,1,2,0:T(8,128)(2,1)}) %all-gather.43.cloned.1.call-update) | async-done | bytes 1572880 | tf_op jit(solution)/shard_map/all_gather | solution.py:147
  115.2 24.1 %reduce-scatter.19.cloned.1.call-done = bf16[152,1,1024]{2,0,1:T(8,128)(2,1)} async-done(((bf16[608,1,1024]{2,0,1:T(8,128)(2,1)}), bf16[152,1,1024]{2,0,1:T(8,128)(2,1)}) %reduce-scatter.19.cloned.1.call-update) | async-done | bytes 311312 | tf_op jit(solution)/shard_map/reduce_scatter | solution.py:179
  144.6 26.2 %all-gather.4 = bf16[1,4096]{1,0:T(2,128)(2,1)S(1)} all-gather(bf16[1,512]{1,0:T(2,128)(2,1)S(1)} %get-tuple-element.227), channel_id=6, replica_groups=mesh['dp'=8,'tensor'=4] {'dp'}, dimensions={1}, use_global_device_ids=true | all-gather | bytes 9216 | tf_op jit(solution)/shard_map/all_gather | solution.py:152
  170.8 20.7 %all-gather.45.cloned.1.call-done = bf16[1,1024,1024]{2,1,0:T(8,128)(2,1)} async-done(((bf16[1,128,1024]{2,1,0:T(8,128)(2,1)}), bf16[1,1024,1024]{2,1,0:T(8,128)(2,1)}) %all-gather.45.cloned.1.call-update) | async-done | bytes 2097168 | tf_op jit(solution)/shard_map/all_gather | solution.py:148
  191.5 18.4 %all-gather.29.cloned.1.call-done = bf16[608,1,1024]{2,0,1:T(8,128)(2,1)} async-done(((bf16[152,1,1024]{2,0,1:T(8,128)(2,1)}), bf16[608,1,1024]{2,0,1:T(8,128)(2,1)}) %all-gather.29.cloned.1.call-update) | async-done | bytes 1245200 | tf_op jit(solution)/shard_map/all_gather | solution.py:193
  209.9 4.8 fusion.26
  214.8 48.9 %all-gather.47.cloned.1.call-done = bf16[1,1024,1024]{2,1,0:T(8,128)(2,1)} async-done(((bf16[1,1024,128]{2,1,0:T(8,128)(2,1)}), bf16[1,1024,1024]{2,1,0:T(8,128)(2,1)}) %all-gather.47.cloned.1.call-update) | async-done | bytes 2097168 | tf_op jit(solution)/shard_map/all_gather | solution.py:150
  263.7 4.9 fusion.58
  269.4 23.6 %reduce-scatter.21.cloned.1.call-done = bf16[152,1,1024]{2,0,1:T(8,128)(2,1)} async-done(((bf16[608,1,1024]{2,0,1:T(8,128)(2,1)}), bf16[152,1,1024]{2,0,1:T(8,128)(2,1)}) %reduce-scatter.21.cloned.1.call-update) | async-done | bytes 311312 | tf_op jit(solution)/shard_map/reduce_scatter | solution.py:217
  295.5 30.8 %all-gather.8 = bf16[1,256,1024]{2,1,0:T(8,128)(2,1)} all-gather(bf16[1,256,128]{2,1,0:T(8,128)(2,1)S(1)} %get-tuple-element.200), channel_id=10, replica_groups=mesh['dp'=8,'tensor'=4] {'dp'}, dimensions={2}, use_global_device_ids=true | all-gather | bytes 589824 | tf_op jit(solution)/shard_map/all_gather | solution.py:149
  326.3 15.3 all-gather.49.cloned.1.call-done
  341.6 18.8 %all-gather.31.cloned.1.call-done = bf16[608,1,1024]{2,0,1:T(8,128)(2,1)} async-done(((bf16[152,1,1024]{2,0,1:T(8,128)(2,1)}), bf16[608,1,1024]{2,0,1:T(8,128)(2,1)}) %all-gather.31.cloned.1.call-update) | async-done | bytes 1245200 | tf_op jit(solution)/shard_map/all_gather | solution.py:171
  374.3 25.5 %reduce-scatter.23.cloned.1.call-done = bf16[152,1,1024]{2,0,1:T(8,128)(2,1)} async-done(((bf16[608,1,1024]{2,0,1:T(8,128)(2,1)}), bf16[152,1,1024]{2,0,1:T(8,128)(2,1)}) %reduce-scatter.23.cloned.1.call-update) | async-done | bytes 311312 | tf_op jit(solution)/shard_map/reduce_scatter | solution.py:179
  404.4 26.2 %all-gather.10 = bf16[1,4096]{1,0:T(2,128)(2,1)S(1)} all-gather(bf16[1,512]{1,0:T(2,128)(2,1)S(1)} %get-tuple-element.226), channel_id=12, replica_groups=mesh['dp'=8,'tensor'=4] {'dp'}, dimensions={1}, use_global_device_ids=true | all-gather | bytes 9216 | tf_op jit(solution)/shard_map/all_gather | solution.py:152
  430.6 21.5 %all-gather.51.cloned.1.call-done = bf16[1,1024,1024]{2,1,0:T(8,128)(2,1)} async-done(((bf16[1,128,1024]{2,1,0:T(8,128)(2,1)}), bf16[1,1024,1024]{2,1,0:T(8,128)(2,1)}) %all-gather.51.cloned.1.call-update) | async-done | bytes 2097168 | tf_op jit(solution)/shard_map/all_gather | solution.py:148
  452.1 18.4 %all-gather.33.cloned.1.call-done = bf16[608,1,1024]{2,0,1:T(8,128)(2,1)} async-done(((bf16[152,1,1024]{2,0,1:T(8,128)(2,1)}), bf16[608,1,1024]{2,0,1:T(8,128)(2,1)}) %all-gather.33.cloned.1.call-update) | async-done | bytes 1245200 | tf_op jit(solution)/shard_map/all_gather | solution.py:193
  470.5 4.9 fusion.18
  475.4 15.2 all-gather.35.cloned.1.call-done
  490.6 53.2 %all-gather.53.cloned.1.call-done = bf16[1,1024,1024]{2,1,0:T(8,128)(2,1)} async-done(((bf16[1,1024,128]{2,1,0:T(8,128)(2,1)}), bf16[1,1024,1024]{2,1,0:T(8,128)(2,1)}) %all-gather.53.cloned.1.call-update) | async-done | bytes 2097168 | tf_op jit(solution)/shard_map/all_gather | solution.py:150
  543.8 5.6 convert_reduce_fusion
  553.2 4.9 fusion.52
  558.3 19.3 %reduce-scatter.27.cloned.1.call-done = bf16[152,1,1024]{2,0,1:T(8,128)(2,1)} async-done(((bf16[608,1,1024]{2,0,1:T(8,128)(2,1)}), bf16[152,1,1024]{2,0,1:T(8,128)(2,1)}) %reduce-scatter.27.cloned.1.call-update) | async-done | bytes 311312 | tf_op jit(solution)/shard_map/reduce_scatter | solution.py:264
  579.5 26.6 %reduce-scatter.25.cloned.1.call-done = bf16[152,1,1024]{2,0,1:T(8,128)(2,1)} async-done(((bf16[608,1,1024]{2,0,1:T(8,128)(2,1)}), bf16[152,1,1024]{2,0,1:T(8,128)(2,1)}) %reduce-scatter.25.cloned.1.call-update) | async-done | bytes 311312 | tf_op jit(solution)/shard_map/reduce_scatter | solution.py:217
  610.6 17.9 %all-gather.37.cloned.1.call-done = bf16[608,1,1024]{2,0,1:T(8,128)(2,1)} async-done(((bf16[152,1,1024]{2,0,1:T(8,128)(2,1)}), bf16[608,1,1024]{2,0,1:T(8,128)(2,1)}) %all-gather.37.cloned.1.call-update) | async-done | bytes 1245200 | tf_op jit(solution)/shard_map/all_gather | solution.py:277
  650.8 26.2 %reduce-scatter.29.cloned.1.call-done = bf16[152,1,1024]{2,0,1:T(8,128)(2,1)} async-done(((bf16[608,1,1024]{2,0,1:T(8,128)(2,1)}), bf16[152,1,1024]{2,0,1:T(8,128)(2,1)}) %reduce-scatter.29.cloned.1.call-update) | async-done | bytes 311312 | tf_op jit(solution)/shard_map/reduce_scatter | solution.py:294
  681.1 17.9 %all-gather.39.cloned.1.call-done = bf16[608,1,1024]{2,0,1:T(8,128)(2,1)} async-done(((bf16[152,1,1024]{2,0,1:T(8,128)(2,1)}), bf16[608,1,1024]{2,0,1:T(8,128)(2,1)}) %all-gather.39.cloned.1.call-update) | async-done | bytes 1245200 | tf_op jit(solution)/shard_map/all_gather | solution.py:251
  699.0 5.6 convert_reduce_fusion.1
  707.6 26.0 %reduce-scatter.31.cloned.1.call-done = bf16[152,1,1024]{2,0,1:T(8,128)(2,1)} async-done(((bf16[608,1,1024]{2,0,1:T(8,128)(2,1)}), bf16[152,1,1024]{2,0,1:T(8,128)(2,1)}) %reduce-scatter.31.cloned.1.call-update) | async-done | bytes 311312 | tf_op jit(solution)/shard_map/reduce_scatter | solution.py:264
  738.3 17.9 %all-gather.41.cloned.1.call-done = bf16[608,1,1024]{2,0,1:T(8,128)(2,1)} async-done(((bf16[152,1,1024]{2,0,1:T(8,128)(2,1)}), bf16[608,1,1024]{2,0,1:T(8,128)(2,1)}) %all-gather.41.cloned.1.call-update) | async-done | bytes 1245200 | tf_op jit(solution)/shard_map/all_gather | solution.py:277
  781.6 18.7 %reduce-scatter.33.cloned.1.call-done = bf16[152,1,1024]{2,0,1:T(8,128)(2,1)} async-done(((bf16[608,1,1024]{2,0,1:T(8,128)(2,1)}), bf16[152,1,1024]{2,0,1:T(8,128)(2,1)}) %reduce-scatter.33.cloned.1.call-update) | async-done | bytes 311312 | tf_op jit(solution)/shard_map/reduce_scatter | solution.py:294
  802.5 5.9 fusion.85
  809.7 5.6 fusion.78
  816.6 5.2 fusion.88
  823.1 5.1 fusion.94
  840.1 37.1 %all-reduce.2 = (f32[4096]{0:T(1024)S(1)}, f32[4096]{0:T(1024)S(1)}) all-reduce(f32[4096]{0:T(1024)S(1)} %dynamic_update_slice.32, f32[4096]{0:T(1024)S(1)} %dynamic_update_slice.31), channel_id=31, replica_groups=mesh['dp'=8,'tensor'=4] {'dp'}, use_global_device_ids=true, to_apply=%region_56.57.clone | all-reduce | flops 8192 | bytes 65536
  877.4 58.0 %reduce-scatter.43.cloned.1.call-done = f32[256,128]{1,0:T(8,128)} async-done(((f32[256,1024]{1,0:T(8,128)}), f32[256,128]{1,0:T(8,128)}) %reduce-scatter.43.cloned.1.call-update) | async-done | bytes 131088 | tf_op jit(solution)/shard_map/reduce_scatter | solution.py:334
  938.8 52.3 %reduce-scatter.37.cloned.1.call-done = f32[8,128]{1,0:T(8,128)} async-done(((f32[8,1024]{1,0:T(8,128)}), f32[8,128]{1,0:T(8,128)}) %reduce-scatter.37.cloned.1.call-update) | async-done | bytes 4112 | tf_op jit(solution)/shard_map/reduce_scatter | solution.py:336
  991.1 55.5 %reduce-scatter.35.cloned.1.call-done = f32[8,128]{1,0:T(8,128)} async-done(((f32[8,1024]{1,0:T(8,128)}), f32[8,128]{1,0:T(8,128)}) %reduce-scatter.35.cloned.1.call-update) | async-done | bytes 4112 | tf_op jit(solution)/shard_map/reduce_scatter | solution.py:336
  1047.3 10.7 all-reduce.3
  1058.6 78.8 %reduce-scatter.53.cloned.1.call-done = f32[1024,128]{1,0:T(8,128)} async-done(((f32[1024,1024]{1,0:T(8,128)}), f32[1024,128]{1,0:T(8,128)}) %reduce-scatter.53.cloned.1.call-update) | async-done | bytes 524304 | tf_op jit(solution)/shard_map/reduce_scatter | solution.py:335
  1137.4 92.2 %reduce-scatter.51.cloned.1.call-done = f32[1024,128]{1,0:T(8,128)} async-done(((f32[1024,1024]{1,0:T(8,128)}), f32[1024,128]{1,0:T(8,128)}) %reduce-scatter.51.cloned.1.call-update) | async-done | bytes 524304 | tf_op jit(solution)/shard_map/reduce_scatter | solution.py:335
  1231.8 89.3 %reduce-scatter.49.cloned.1.call-done = f32[128,1024]{1,0:T(8,128)} async-done(((f32[1024,1024]{1,0:T(8,128)}), f32[128,1024]{1,0:T(8,128)}) %reduce-scatter.49.cloned.1.call-update) | async-done | bytes 524304 | tf_op jit(solution)/shard_map/reduce_scatter | solution.py:333
  1321.1 91.6 %reduce-scatter.47.cloned.1.call-done = f32[128,1024]{1,0:T(8,128)} async-done(((f32[1024,1024]{1,0:T(8,128)}), f32[128,1024]{1,0:T(8,128)}) %reduce-scatter.47.cloned.1.call-update) | async-done | bytes 524304 | tf_op jit(solution)/shard_map/reduce_scatter | solution.py:333
  1415.0 76.0 %reduce-scatter.41.cloned.1.call-done = f32[128,3,256]{2,0,1:T(8,128)} async-done(((f32[1024,3,256]{2,0,1:T(8,128)}), f32[128,3,256]{2,0,1:T(8,128)}) %reduce-scatter.41.cloned.1.call-update) | async-done | bytes 393232 | tf_op jit(solution)/shard_map/reduce_scatter | solution.py:332
  1491.0 77.7 %reduce-scatter.39.cloned.1.call-done = f32[128,3,256]{2,0,1:T(8,128)} async-done(((f32[1024,3,256]{2,0,1:T(8,128)}), f32[128,3,256]{2,0,1:T(8,128)}) %reduce-scatter.39.cloned.1.call-update) | async-done | bytes 393232 | tf_op jit(solution)/shard_map/reduce_scatter | solution.py:332
  (385 shorter events, 147.7 us)
Async XLA Ops:
  7.2 50.7 %copy-start.69 = (s32[608,1]{0,1:T(1,128)S(1)}, s32[608,1]{0,1:T(1,128)}, u32[]{:S(2)}) copy-start(s32[608,1]{0,1:T(1,128)} %param.33) | copy-start | bytes 7300
  7.2 50.8 %copy-start.36 = (bf16[2,256,128]{2,1,0:T(8,128)(2,1)S(1)}, bf16[2,256,128]{2,1,0:T(8,128)(2,1)}, u32[]{:S(2)}) copy-start(bf16[2,256,128]{2,1,0:T(8,128)(2,1)} %param.23) | copy-start | bytes 393220
  7.2 79.0 %all-gather.27.cloned.1.call-start = ((), (), s32[]{:S(2)}) async-start(), calls=%async_computation.18 | async-start | bytes 1556480 | tf_op jit(solution)/shard_map/all_gather | solution.py:171
  8.4 97.5 %copy-start.47 = (f32[152]{0:T(256)}, f32[152]{0:T(256)S(1)}, u32[]{:S(2)}) copy-start(f32[152]{0:T(256)S(1)} %broadcast_multiply_fusion.11) | copy-start | bytes 1828
  9.6 96.3 %copy-start.53 = (f32[152]{0:T(256)}, f32[152]{0:T(256)S(1)}, u32[]{:S(2)}) copy-start(f32[152]{0:T(256)S(1)} %add_rsqrt_fusion.3) | copy-start | bytes 1828
  37.4 68.6 %copy-start.39 = (f32[1,1,1024]{2,0,1:T(1,128)}, f32[1,1,1024]{2,0,1:T(1,128)S(1)}, u32[]{:S(2)}) copy-start(f32[1,1,1024]{2,0,1:T(1,128)S(1)} %get-tuple-element.211) | copy-start | bytes 12292
  37.4 104.3 %copy-start.43 = (f32[1,1,1024]{2,0,1:T(1,128)}, f32[1,1,1024]{2,0,1:T(1,128)S(1)}, u32[]{:S(2)}) copy-start(f32[1,1,1024]{2,0,1:T(1,128)S(1)} %get-tuple-element.214) | copy-start | bytes 12292
  39.3 63.6 %all-gather.43.cloned.1.call-start = ((), (), s32[]{:S(2)}) async-start(), calls=%async_computation.44 | async-start | bytes 1769472 | tf_op jit(solution)/shard_map/all_gather | solution.py:147
  41.2 98.1 %reduce-scatter.19.cloned.1.call-start = ((), (), s32[]{:S(2)}) async-start(), calls=%async_computation.19 | async-start | bytes 1556480 | tf_op jit(solution)/shard_map/reduce_scatter | solution.py:179
  57.9 236.6 %copy-start.41 = (f32[1,1,1024]{2,0,1:T(1,128)}, f32[1,1,1024]{2,0,1:T(1,128)S(1)}, u32[]{:S(2)}) copy-start(f32[1,1,1024]{2,0,1:T(1,128)S(1)} %get-tuple-element.207) | copy-start | bytes 12292
  114.3 77.2 %all-gather.45.cloned.1.call-start = ((), (), s32[]{:S(2)}) async-start(), calls=%async_computation.45 | async-start | bytes 2359296 | tf_op jit(solution)/shard_map/all_gather | solution.py:148
  115.2 94.7 %all-gather.29.cloned.1.call-start = ((), (), s32[]{:S(2)}) async-start(), calls=%async_computation.20 | async-start | bytes 1556480 | tf_op jit(solution)/shard_map/all_gather | solution.py:193
  140.5 74.3 %copy-start.51 = (f32[152]{0:T(256)}, f32[152]{0:T(256)S(1)}, u32[]{:S(2)}) copy-start(f32[152]{0:T(256)S(1)} %broadcast_multiply_fusion.10) | copy-start | bytes 1828
  141.7 73.0 %copy-start.66 = (f32[152]{0:T(256)}, f32[152]{0:T(256)S(1)}, u32[]{:S(2)}) copy-start(f32[152]{0:T(256)S(1)} %add_rsqrt_fusion.2) | copy-start | bytes 1828
  143.6 120.0 %all-gather.47.cloned.1.call-start = ((), (), s32[]{:S(2)}) async-start(), calls=%async_computation.46 | async-start | bytes 2359296 | tf_op jit(solution)/shard_map/all_gather | solution.py:150
  144.5 148.5 %reduce-scatter.21.cloned.1.call-start = ((), (), s32[]{:S(2)}) async-start(), calls=%async_computation.21 | async-start | bytes 1556480 | tf_op jit(solution)/shard_map/reduce_scatter | solution.py:217
  170.8 92.9 %copy-start.70 = (f32[1,1024]{1,0:T(1,128)}, f32[1,1024]{1,0:T(1,128)S(1)}, u32[]{:S(2)}) copy-start(f32[1,1024]{1,0:T(1,128)S(1)} %dynamic-slice_convert_fusion.1) | copy-start | bytes 12292
  268.6 73.0 %all-gather.49.cloned.1.call-start = ((), (), s32[]{:S(2)}) async-start(), calls=%async_computation.47 | async-start | bytes 1769472 | tf_op jit(solution)/shard_map/all_gather | solution.py:147
  269.4 91.0 %all-gather.31.cloned.1.call-start = ((), (), s32[]{:S(2)}) async-start(), calls=%async_computation.22 | async-start | bytes 1556480 | tf_op jit(solution)/shard_map/all_gather | solution.py:171
  294.3 70.0 %copy-start.49 = (f32[152]{0:T(256)}, f32[152]{0:T(256)S(1)}, u32[]{:S(2)}) copy-start(f32[152]{0:T(256)S(1)} %broadcast_multiply_fusion.9) | copy-start | bytes 1828
  294.5 69.7 %copy-start.64 = (f32[152]{0:T(256)}, f32[152]{0:T(256)S(1)}, u32[]{:S(2)}) copy-start(f32[152]{0:T(256)S(1)} %add_rsqrt_fusion.1) | copy-start | bytes 1828
  295.5 104.4 %reduce-scatter.23.cloned.1.call-start = ((), (), s32[]{:S(2)}) async-start(), calls=%async_computation.23 | async-start | bytes 1556480 | tf_op jit(solution)/shard_map/reduce_scatter | solution.py:179
  373.5 78.6 %all-gather.51.cloned.1.call-start = ((), (), s32[]{:S(2)}) async-start(), calls=%async_computation.48 | async-start | bytes 2359296 | tf_op jit(solution)/shard_map/all_gather | solution.py:148
  374.3 96.3 %all-gather.33.cloned.1.call-start = ((), (), s32[]{:S(2)}) async-start(), calls=%async_computation.24 | async-start | bytes 1556480 | tf_op jit(solution)/shard_map/all_gather | solution.py:193
  402.1 88.5 %all-gather.35.cloned.1.call-start = ((), (), s32[]{:S(2)}) async-start(), calls=%async_computation.26 | async-start | bytes 1556480 | tf_op jit(solution)/shard_map/all_gather | solution.py:251
  403.8 140.1 %all-gather.53.cloned.1.call-start = ((), (), s32[]{:S(2)}) async-start(), calls=%async_computation.49 | async-start | bytes 2359296 | tf_op jit(solution)/shard_map/all_gather | solution.py:150
  404.3 173.2 %reduce-scatter.27.cloned.1.call-start = ((), (), s32[]{:S(2)}) async-start(), calls=%async_computation.27 | async-start | bytes 1556480 | tf_op jit(solution)/shard_map/reduce_scatter | solution.py:264
  430.6 122.6 %copy-start.74 = (f32[1,1024]{1,0:T(1,128)}, f32[1,1024]{1,0:T(1,128)S(1)}, u32[]{:S(2)}) copy-start(f32[1,1024]{1,0:T(1,128)S(1)} %dynamic-slice_convert_fusion) | copy-start | bytes 12292
  553.1 53.0 %reduce-scatter.25.cloned.1.call-start = ((), (), s32[]{:S(2)}) async-start(), calls=%async_computation.25 | async-start | bytes 1556480 | tf_op jit(solution)/shard_map/reduce_scatter | solution.py:217
  558.1 70.5 %copy-start.15 = (bf16[1,256,1024]{2,1,0:T(8,128)(2,1)S(1)}, bf16[1,256,1024]{2,1,0:T(8,128)(2,1)}, u32[]{:S(2)}) copy-start(bf16[1,256,1024]{2,1,0:T(8,128)(2,1)} %all-gather.8) | copy-start | bytes 1572868
  558.1 70.5 %all-gather.37.cloned.1.call-start = ((), (), s32[]{:S(2)}) async-start(), calls=%async_computation.28 | async-start | bytes 1556480 | tf_op jit(solution)/shard_map/all_gather | solution.py:277
  610.6 66.5 %reduce-scatter.29.cloned.1.call-start = ((), (), s32[]{:S(2)}) async-start(), calls=%async_computation.29 | async-start | bytes 1556480 | tf_op jit(solution)/shard_map/reduce_scatter | solution.py:294
  650.8 48.2 %all-gather.39.cloned.1.call-start = ((), (), s32[]{:S(2)}) async-start(), calls=%async_computation.30 | async-start | bytes 1556480 | tf_op jit(solution)/shard_map/all_gather | solution.py:251
  681.0 52.5 %reduce-scatter.31.cloned.1.call-start = ((), (), s32[]{:S(2)}) async-start(), calls=%async_computation.31 | async-start | bytes 1556480 | tf_op jit(solution)/shard_map/reduce_scatter | solution.py:264
  707.3 48.9 %copy-start.13 = (bf16[1,256,1024]{2,1,0:T(8,128)(2,1)S(1)}, bf16[1,256,1024]{2,1,0:T(8,128)(2,1)}, u32[]{:S(2)}) copy-start(bf16[1,256,1024]{2,1,0:T(8,128)(2,1)} %copy-done.12) | copy-start | bytes 1572868
  707.3 48.9 %all-gather.41.cloned.1.call-start = ((), (), s32[]{:S(2)}) async-start(), calls=%async_computation.32 | async-start | bytes 1556480 | tf_op jit(solution)/shard_map/all_gather | solution.py:277
  738.2 62.1 %reduce-scatter.33.cloned.1.call-start = ((), (), s32[]{:S(2)}) async-start(), calls=%async_computation.33 | async-start | bytes 1556480 | tf_op jit(solution)/shard_map/reduce_scatter | solution.py:294
  774.1 103.3 %reduce-scatter.45.cloned.1.call-start = ((), (), s32[]{:S(2)}) async-start(), calls=%async_computation.39 | async-start | bytes 1179648 | tf_op jit(solution)/shard_map/reduce_scatter | solution.py:334
  777.1 158.2 %reduce-scatter.43.cloned.1.call-start = ((), (), s32[]{:S(2)}) async-start(), calls=%async_computation.38 | async-start | bytes 1179648 | tf_op jit(solution)/shard_map/reduce_scatter | solution.py:334
  780.1 210.9 %reduce-scatter.37.cloned.1.call-start = ((), (), s32[]{:S(2)}) async-start(), calls=%async_computation.35 | async-start | bytes 36864 | tf_op jit(solution)/shard_map/reduce_scatter | solution.py:336
  781.2 265.4 %reduce-scatter.35.cloned.1.call-start = ((), (), s32[]{:S(2)}) async-start(), calls=%async_computation.34 | async-start | bytes 36864 | tf_op jit(solution)/shard_map/reduce_scatter | solution.py:336
  802.4 335.0 %reduce-scatter.53.cloned.1.call-start = ((), (), s32[]{:S(2)}) async-start(), calls=%async_computation.43 | async-start | bytes 4718592 | tf_op jit(solution)/shard_map/reduce_scatter | solution.py:335
  808.4 421.2 %reduce-scatter.51.cloned.1.call-start = ((), (), s32[]{:S(2)}) async-start(), calls=%async_computation.42 | async-start | bytes 4718592 | tf_op jit(solution)/shard_map/reduce_scatter | solution.py:335
  815.4 505.7 %reduce-scatter.49.cloned.1.call-start = ((), (), s32[]{:S(2)}) async-start(), calls=%async_computation.41 | async-start | bytes 4718592 | tf_op jit(solution)/shard_map/reduce_scatter | solution.py:333
  821.8 590.9 %reduce-scatter.47.cloned.1.call-start = ((), (), s32[]{:S(2)}) async-start(), calls=%async_computation.40 | async-start | bytes 4718592 | tf_op jit(solution)/shard_map/reduce_scatter | solution.py:333
  828.2 662.8 %reduce-scatter.41.cloned.1.call-start = ((), (), s32[]{:S(2)}) async-start(), calls=%async_computation.37 | async-start | bytes 3538944 | tf_op jit(solution)/shard_map/reduce_scatter | solution.py:332
  832.9 735.7 %reduce-scatter.39.cloned.1.call-start = ((), (), s32[]{:S(2)}) async-start(), calls=%async_computation.36 | async-start | bytes 3538944 | tf_op jit(solution)/shard_map/reduce_scatter | solution.py:332
  837.6 99.5 %copy-start.20 = (bf16[152,1,1024]{2,0,1:T(8,128)(2,1)S(1)}, bf16[152,1,1024]{2,0,1:T(8,128)(2,1)}, u32[]{:S(2)}) copy-start(bf16[152,1,1024]{2,0,1:T(8,128)(2,1)} %reduce-scatter.33.cloned.1.call-done) | copy-start | bytes 933892
  (75 other events, 786.9 us)
Sparse Core Ops, SparseCore 0:
  39.5 15.0 all-gather.26
  57.3 45.6 all-gather.42
  114.4 24.9 reduce-scatter.18
  142.1 49.3 all-gather.44
  193.6 16.2 all-gather.28
  212.6 51.0 all-gather.46
  268.8 24.2 reduce-scatter.20
  295.8 45.7 all-gather.48
  343.7 16.6 all-gather.30
  373.7 26.1 reduce-scatter.22
  402.7 49.3 all-gather.50
  454.2 16.2 all-gather.32
  472.7 17.8 all-gather.34
  492.7 51.0 all-gather.52
  553.2 24.3 reduce-scatter.26
  580.0 26.0 reduce-scatter.24
  610.7 17.8 all-gather.36
  650.9 26.1 reduce-scatter.28
  681.1 17.8 all-gather.38
  707.4 26.1 reduce-scatter.30
  738.4 17.8 all-gather.40
  774.2 26.1 reduce-scatter.32
  804.3 63.8 reduce-scatter.44
  872.5 62.8 reduce-scatter.42
  938.5 52.5 reduce-scatter.36
  994.1 52.5 reduce-scatter.34
  1050.1 87.2 reduce-scatter.52
  1141.5 88.0 reduce-scatter.50
  1233.2 87.8 reduce-scatter.48
  1325.0 87.6 reduce-scatter.46
  1416.3 74.5 reduce-scatter.40
  1494.6 73.9 reduce-scatter.38
where the time goes:
time: 1590 us; the launch traced here: 1580 us
  waiting for transfers between devices  1160 us (73%)
  blocking collectives  198 us (12%)
  matrix products  119 us (7%)
  other arithmetic  43.7 us (3%)
  local copies, waits for them, and re-layouts  33.6 us (2%)
  between operations  17.1 us (1%)
    reduce_scatter x2, waiting for transfers between devices, body(): lax.psum_scatter(grad_up_w, 'dp', scatter_dimension=0, tiled=True)  181 us
    reduce_scatter x2, waiting for transfers between devices, body(): lax.psum_scatter(grad_down_w, 'dp', scatter_dimension=1, tiled=True)  171 us
    reduce_scatter x2, waiting for transfers between devices, body(): lax.psum_scatter(grad_qkv_w, 'dp', scatter_dimension=0, tiled=True)  154 us
    reduce_scatter x2, waiting for transfers between devices, body(): lax.psum_scatter(grad_vec, 'dp', scatter_dimension=1, tiled=True)  108 us
    all_gather x2, waiting for transfers between devices, fetch(): lax.all_gather(down_weight[depth], 'dp', axis=1, tiled=True)  102 us
    all_gather x2, blocking collectives, fetch(): lax.all_gather(out_weight[depth], 'dp', axis=1, tiled=True)  58.9 us
    reduce_scatter x2, waiting for transfers between devices, body(): lax.psum_scatter(grad_out_w, 'dp', scatter_dimension=1, tiled=True)  58 us
    all_gather x2, blocking collectives, fetch(): lax.all_gather(up_bias[depth], 'dp', axis=0, tiled=True)  52.4 us
  transfers between devices with their start and end apart: 32, of which 30 were waited for; matrix products, arithmetic and copies ran while one was open for 5% of the time, Pallas kernels for 0%

commit v1 on v0

--- a/solution.py
+++ b/solution.py
@@ -229,8 +229,8 @@
     grad = cotangent.astype(jnp.float32) * live[:, :, None]
     per_layer = []
     for depth in reversed(range(depth_count)):
-        weights = fetch(depth)
-        parts = forward_parts(layer_inputs[depth], weights)
+        weights = kept[depth]
+        parts = stored[depth]
         layer_qkv_w = weights[0]
         layer_up_w = weights[1]
         layer_out_w = weights[2]
@@ -251,7 +251,7 @@
         fold_piece = lax.all_gather(grad.astype(jnp.bfloat16), "tensor", axis=0, tiled=True)
         update = jnp.einsum("sid,fd->sif", fold_piece, down_w, preferred_element_type=jnp.float32)
         grad_down_w = jnp.einsum(
-            "sif,sid->fd", layer_active, fold_piece, preferred_element_type=jnp.float32
+            "sif,sid->df", layer_active, fold_piece, preferred_element_type=jnp.float32
         )
         grad_before = (update * gelu_slope(layer_before)).astype(jnp.bfloat16)
         grad_up_cols = jnp.sum(grad_before.astype(jnp.float32), (0, 1))
@@ -279,7 +279,7 @@
             "sid,ed->sie", piece, layer_out_w, preferred_element_type=jnp.float32
         )
         grad_out_w = jnp.einsum(
-            "sie,sid->ed", layer_mixed, piece, preferred_element_type=jnp.float32
+            "sie,sid->de", layer_mixed, piece, preferred_element_type=jnp.float32
         )
         grad_qkv = attention_backward(
             layer_qkv, layer_lses, fold_update.astype(jnp.bfloat16), row_mask
@@ -328,19 +328,40 @@
                 grad_down_bias,
             ]
         )
+        flat = jnp.concatenate(
+            [
+                grad_qkv_w.reshape(grad_qkv_w.shape[0], -1),
+                grad_up_w,
+                grad_out_w,
+                grad_down_w,
+            ],
+            1,
+        ).astype(jnp.bfloat16)
+        flat = lax.psum_scatter(flat, "dp", scatter_dimension=0, tiled=True).astype(jnp.float32)
+        ends = [3 * head_width, 3 * head_width + unit_width, 4 * head_width + unit_width]
+        part_qkv, part_up, part_out, part_down = jnp.split(flat, ends, 1)
         shards = (
-            lax.psum_scatter(grad_qkv_w, "dp", scatter_dimension=0, tiled=True),
-            lax.psum_scatter(grad_up_w, "dp", scatter_dimension=0, tiled=True),
-            lax.psum_scatter(grad_out_w, "dp", scatter_dimension=1, tiled=True),
-            lax.psum_scatter(grad_down_w, "dp", scatter_dimension=1, tiled=True),
-            lax.psum_scatter(grad_vec, "dp", scatter_dimension=1, tiled=True),
-            lax.psum_scatter(grad_up_full, "dp", scatter_dimension=0, tiled=True),
-        )
-        grad, shards = (grad_in, shards)
+            part_qkv.reshape(-1, 3, head_width),
+            part_up,
+            part_out.T,
+            part_down.T,
+            grad_vec,
+            grad_up_full,
+        )
+        grad = grad_in
         per_layer.insert(0, shards)
     vec_grads = jnp.stack([shards[4] for shards in per_layer])
     bias_grads = jnp.stack([shards[5] for shards in per_layer])
-    vec_sum, up_sum = lax.psum((vec_grads, bias_grads), "tensor")
+    whole_vec = jnp.concatenate([vec_grads, bias_grads.reshape(depth_count, -1, full_width)], 1)
+    whole_vec = lax.psum(whole_vec, ("dp", "tensor"))
+    dp_rank = lax.axis_index("dp")
+    shard_width = attn_gain.shape[1]
+    vec_sum = lax.dynamic_slice_in_dim(
+        whole_vec[:, :8], dp_rank * shard_width, shard_width, 2
+    )
+    up_sum = lax.dynamic_slice_in_dim(
+        whole_vec[:, 8:].reshape(depth_count, -1), dp_rank * up_bias.shape[1], up_bias.shape[1], 1
+    )
     return (
         hidden.astype(jnp.bfloat16),
         grad,

time: 1590 us -> 1200 us (0.75)
  waiting for transfers between devices: 1160 us -> 800 us
  blocking collectives: 198 us -> 149 us
  local copies, waits for them, and re-layouts: 33.6 us -> 59.1 us
    reduce_scatter x10 -> x0, waiting for transfers between devices: 671 us -> none  [the longest x2 181 us: body(): lax.psum_scatter(grad_up_w, 'dp', scatter_dimension=0, tiled=True)]
    unnamed x32 -> x27, waiting for transfers between devices: 2.38 us -> 239 us
    psum x0 -> x1, waiting for transfers between devices: none -> 80.5 us  [body(): whole_vec = lax.psum(whole_vec, ('dp', 'tensor'))]
    unnamed x1 -> x0, blocking collectives: 37.1 us -> none
    unnamed x193 -> x169, local copies, waits for them, and re-layouts: 21 us -> 36.5 us
  transfers between devices with their start and end apart: 32 -> 25, of which waited for: 30 -> 24; matrix products, arithmetic and copies ran while one was open for 5% -> 8% of each run, Pallas kernels for 0% -> 0%
where the time goes in v1:
time: 1200 us; the launch traced here: 1190 us
  waiting for transfers between devices  800 us (67%)
  blocking collectives  149 us (12%)
  matrix products  117 us (10%)
  local copies, waits for them, and re-layouts  59.1 us (5%)
  other arithmetic  51.9 us (4%)
  between operations  16.2 us (1%)
    unnamed x27, waiting for transfers between devices  239 us
    all_gather x2, waiting for transfers between devices, fetch(): lax.all_gather(down_weight[depth], 'dp', axis=1, tiled=True)  102 us
    psum x1, waiting for transfers between devices, body(): whole_vec = lax.psum(whole_vec, ('dp', 'tensor'))  80.5 us
    all_gather x2, blocking collectives, fetch(): lax.all_gather(out_weight[depth], 'dp', axis=1, tiled=True)  57.6 us
    all_gather x2, blocking collectives, fetch(): lax.all_gather(up_bias[depth], 'dp', axis=0, tiled=True)  52.4 us
    reduce_scatter x2, waiting for transfers between devices, forward_parts(): lax.psum_scatter(jnp.einsum('sie,ed->sid', mixed, out_w, preferred_elemen...  49.6 us
    reduce_scatter x2, waiting for transfers between devices, body(): lax.psum_scatter(jnp.einsum('sif,fd->sid', mlp_active, mlp_down_w, prefer...  49.2 us
    reduce_scatter x2, waiting for transfers between devices, body(): lax.psum_scatter(jnp.einsum('sif,df->sid', grad_before, layer_up_w, prefe...  44.4 us
  transfers between devices with their start and end apart: 25, of which 24 were waited for; matrix products, arithmetic and copies ran while one was open for 8% of the time, Pallas kernels for 0%

profile of v1, /device:TPU:0, one launch (start us, length us, event | category | flops | bytes accessed | tf_op | source)
XLA Modules:
  0.0 1194.4 jit_solution(9559652890281156475)
XLA Ops:
  14.9 22.4 %all-gather = bf16[1,8,1024]{2,0,1:T(2,128)(2,1)S(1)} all-gather(bf16[1,8,128]{2,0,1:T(2,128)(2,1)S(1)} %get-tuple-element.196), channel_id=2, replica_groups=mesh['dp'=8,'tensor'=4] {'dp'}, dimensions={2}, use_global_device_ids=true | all-gather | bytes 18432 | tf_op jit(solution)/shard_map/all_gather | solution.py:151
  41.3 16.5 %all-gather.6 = bf16[1,8,1024]{2,0,1:T(2,128)(2,1)S(1)} all-gather(bf16[1,8,128]{2,0,1:T(2,128)(2,1)S(1)} %get-tuple-element.197), channel_id=8, replica_groups=mesh['dp'=8,'tensor'=4] {'dp'}, dimensions={2}, use_global_device_ids=true | all-gather | bytes 18432 | tf_op jit(solution)/shard_map/all_gather | solution.py:151
  58.0 28.1 %all-gather.2 = bf16[1,256,1024]{2,1,0:T(8,128)(2,1)S(1)} all-gather(bf16[1,256,128]{2,1,0:T(8,128)(2,1)S(1)} %get-tuple-element.173), channel_id=4, replica_groups=mesh['dp'=8,'tensor'=4] {'dp'}, dimensions={2}, use_global_device_ids=true | all-gather | bytes 589824 | tf_op jit(solution)/shard_map/all_gather | solution.py:149
  86.1 16.8 %all-gather.43.cloned.1.call-done = bf16[1,1024,3,256]{3,1,2,0:T(8,128)(2,1)} async-done(((bf16[1,128,3,256]{3,1,2,0:T(8,128)(2,1)}), bf16[1,1024,3,256]{3,1,2,0:T(8,128)(2,1)}) %all-gather.43.cloned.1.call-update) | async-done | bytes 1572880 | tf_op jit(solution)/shard_map/all_gather | solution.py:147
  114.5 24.1 %reduce-scatter.15.cloned.1.call-done = bf16[152,1,1024]{2,0,1:T(8,128)(2,1)} async-done(((bf16[608,1,1024]{2,0,1:T(8,128)(2,1)}), bf16[152,1,1024]{2,0,1:T(8,128)(2,1)}) %reduce-scatter.15.cloned.1.call-update) | async-done | bytes 311312 | tf_op jit(solution)/shard_map/reduce_scatter | solution.py:179
  143.8 26.2 %all-gather.4 = bf16[1,4096]{1,0:T(2,128)(2,1)S(1)} all-gather(bf16[1,512]{1,0:T(2,128)(2,1)S(1)} %get-tuple-element.199), channel_id=6, replica_groups=mesh['dp'=8,'tensor'=4] {'dp'}, dimensions={1}, use_global_device_ids=true | all-gather | bytes 9216 | tf_op jit(solution)/shard_map/all_gather | solution.py:152
  170.0 20.7 %all-gather.45.cloned.1.call-done = bf16[1,1024,1024]{2,1,0:T(8,128)(2,1)} async-done(((bf16[1,128,1024]{2,1,0:T(8,128)(2,1)}), bf16[1,1024,1024]{2,1,0:T(8,128)(2,1)}) %all-gather.45.cloned.1.call-update) | async-done | bytes 2097168 | tf_op jit(solution)/shard_map/all_gather | solution.py:148
  190.7 18.4 %all-gather.29.cloned.1.call-done = bf16[608,1,1024]{2,0,1:T(8,128)(2,1)} async-done(((bf16[152,1,1024]{2,0,1:T(8,128)(2,1)}), bf16[608,1,1024]{2,0,1:T(8,128)(2,1)}) %all-gather.29.cloned.1.call-update) | async-done | bytes 1245200 | tf_op jit(solution)/shard_map/all_gather | solution.py:193
  209.1 4.9 fusion.26
  214.0 48.9 %all-gather.47.cloned.1.call-done = bf16[1,1024,1024]{2,1,0:T(8,128)(2,1)} async-done(((bf16[1,1024,128]{2,1,0:T(8,128)(2,1)}), bf16[1,1024,1024]{2,1,0:T(8,128)(2,1)}) %all-gather.47.cloned.1.call-update) | async-done | bytes 2097168 | tf_op jit(solution)/shard_map/all_gather | solution.py:150
  262.9 4.9 fusion.58
  268.6 23.6 %reduce-scatter.17.cloned.1.call-done = bf16[152,1,1024]{2,0,1:T(8,128)(2,1)} async-done(((bf16[608,1,1024]{2,0,1:T(8,128)(2,1)}), bf16[152,1,1024]{2,0,1:T(8,128)(2,1)}) %reduce-scatter.17.cloned.1.call-update) | async-done | bytes 311312 | tf_op jit(solution)/shard_map/reduce_scatter | solution.py:217
  294.7 29.5 %all-gather.8 = bf16[1,256,1024]{2,1,0:T(8,128)(2,1)S(1)} all-gather(bf16[1,256,128]{2,1,0:T(8,128)(2,1)S(1)} %get-tuple-element.172), channel_id=10, replica_groups=mesh['dp'=8,'tensor'=4] {'dp'}, dimensions={2}, use_global_device_ids=true | all-gather | bytes 589824 | tf_op jit(solution)/shard_map/all_gather | solution.py:149
  324.2 16.9 %all-gather.49.cloned.1.call-done = bf16[1,1024,3,256]{3,1,2,0:T(8,128)(2,1)} async-done(((bf16[1,128,3,256]{3,1,2,0:T(8,128)(2,1)}), bf16[1,1024,3,256]{3,1,2,0:T(8,128)(2,1)}) %all-gather.49.cloned.1.call-update) | async-done | bytes 1572880 | tf_op jit(solution)/shard_map/all_gather | solution.py:147
  341.1 18.8 %all-gather.31.cloned.1.call-done = bf16[608,1,1024]{2,0,1:T(8,128)(2,1)} async-done(((bf16[152,1,1024]{2,0,1:T(8,128)(2,1)}), bf16[608,1,1024]{2,0,1:T(8,128)(2,1)}) %all-gather.31.cloned.1.call-update) | async-done | bytes 1245200 | tf_op jit(solution)/shard_map/all_gather | solution.py:171
  359.9 3.8 add_convert_fusion
  376.5 25.5 %reduce-scatter.19.cloned.1.call-done = bf16[152,1,1024]{2,0,1:T(8,128)(2,1)} async-done(((bf16[608,1,1024]{2,0,1:T(8,128)(2,1)}), bf16[152,1,1024]{2,0,1:T(8,128)(2,1)}) %reduce-scatter.19.cloned.1.call-update) | async-done | bytes 311312 | tf_op jit(solution)/shard_map/reduce_scatter | solution.py:179
  406.6 26.2 %all-gather.10 = bf16[1,4096]{1,0:T(2,128)(2,1)S(1)} all-gather(bf16[1,512]{1,0:T(2,128)(2,1)S(1)} %get-tuple-element.198), channel_id=12, replica_groups=mesh['dp'=8,'tensor'=4] {'dp'}, dimensions={1}, use_global_device_ids=true | all-gather | bytes 9216 | tf_op jit(solution)/shard_map/all_gather | solution.py:152
  432.8 21.5 %all-gather.51.cloned.1.call-done = bf16[1,1024,1024]{2,1,0:T(8,128)(2,1)} async-done(((bf16[1,128,1024]{2,1,0:T(8,128)(2,1)}), bf16[1,1024,1024]{2,1,0:T(8,128)(2,1)}) %all-gather.51.cloned.1.call-update) | async-done | bytes 2097168 | tf_op jit(solution)/shard_map/all_gather | solution.py:148
  454.3 18.4 %all-gather.33.cloned.1.call-done = bf16[608,1,1024]{2,0,1:T(8,128)(2,1)} async-done(((bf16[152,1,1024]{2,0,1:T(8,128)(2,1)}), bf16[608,1,1024]{2,0,1:T(8,128)(2,1)}) %all-gather.33.cloned.1.call-update) | async-done | bytes 1245200 | tf_op jit(solution)/shard_map/all_gather | solution.py:193
  472.7 4.9 fusion.18
  477.6 15.2 %all-gather.35.cloned.1.call-done = bf16[608,1,1024]{2,0,1:T(8,128)(2,1)} async-done(((bf16[152,1,1024]{2,0,1:T(8,128)(2,1)}), bf16[608,1,1024]{2,0,1:T(8,128)(2,1)}) %all-gather.35.cloned.1.call-update) | async-done | bytes 1245200 | tf_op jit(solution)/shard_map/all_gather | solution.py:251
  492.8 53.2 %all-gather.53.cloned.1.call-done = bf16[1,1024,1024]{2,1,0:T(8,128)(2,1)} async-done(((bf16[1,1024,128]{2,1,0:T(8,128)(2,1)}), bf16[1,1024,1024]{2,1,0:T(8,128)(2,1)}) %all-gather.53.cloned.1.call-update) | async-done | bytes 2097168 | tf_op jit(solution)/shard_map/all_gather | solution.py:150
  546.0 5.6 convert_reduce_fusion
  555.4 4.9 fusion.52
  561.4 18.4 %reduce-scatter.23.cloned.1.call-done = bf16[152,1,1024]{2,0,1:T(8,128)(2,1)} async-done(((bf16[608,1,1024]{2,0,1:T(8,128)(2,1)}), bf16[152,1,1024]{2,0,1:T(8,128)(2,1)}) %reduce-scatter.23.cloned.1.call-update) | async-done | bytes 311312 | tf_op jit(solution)/shard_map/reduce_scatter | solution.py:264
  582.8 25.5 %reduce-scatter.21.cloned.1.call-done = bf16[152,1,1024]{2,0,1:T(8,128)(2,1)} async-done(((bf16[608,1,1024]{2,0,1:T(8,128)(2,1)}), bf16[152,1,1024]{2,0,1:T(8,128)(2,1)}) %reduce-scatter.21.cloned.1.call-update) | async-done | bytes 311312 | tf_op jit(solution)/shard_map/reduce_scatter | solution.py:217
  612.1 17.9 %all-gather.37.cloned.1.call-done = bf16[608,1,1024]{2,0,1:T(8,128)(2,1)} async-done(((bf16[152,1,1024]{2,0,1:T(8,128)(2,1)}), bf16[608,1,1024]{2,0,1:T(8,128)(2,1)}) %all-gather.37.cloned.1.call-update) | async-done | bytes 1245200 | tf_op jit(solution)/shard_map/all_gather | solution.py:277
  633.9 4.7 fusion.99
  638.6 4.4 multiply_reduce_fusion.1
  652.8 3.8 fusion.46
  656.8 26.2 %reduce-scatter.25.cloned.1.call-done = bf16[152,1,1024]{2,0,1:T(8,128)(2,1)} async-done(((bf16[608,1,1024]{2,0,1:T(8,128)(2,1)}), bf16[152,1,1024]{2,0,1:T(8,128)(2,1)}) %reduce-scatter.25.cloned.1.call-update) | async-done | bytes 311312 | tf_op jit(solution)/shard_map/reduce_scatter | solution.py:294
  687.0 17.9 %all-gather.39.cloned.1.call-done = bf16[608,1,1024]{2,0,1:T(8,128)(2,1)} async-done(((bf16[152,1,1024]{2,0,1:T(8,128)(2,1)}), bf16[608,1,1024]{2,0,1:T(8,128)(2,1)}) %all-gather.39.cloned.1.call-update) | async-done | bytes 1245200 | tf_op jit(solution)/shard_map/all_gather | solution.py:251
  705.0 5.6 convert_reduce_fusion.1
  714.5 26.0 %reduce-scatter.27.cloned.1.call-done = bf16[152,1,1024]{2,0,1:T(8,128)(2,1)} async-done(((bf16[608,1,1024]{2,0,1:T(8,128)(2,1)}), bf16[152,1,1024]{2,0,1:T(8,128)(2,1)}) %reduce-scatter.27.cloned.1.call-update) | async-done | bytes 311312 | tf_op jit(solution)/shard_map/reduce_scatter | solution.py:264
  745.3 5.3 convolution_convert_fusion
  750.6 12.6 %all-gather.41.cloned.1.call-done = bf16[608,1,1024]{2,0,1:T(8,128)(2,1)} async-done(((bf16[152,1,1024]{2,0,1:T(8,128)(2,1)}), bf16[608,1,1024]{2,0,1:T(8,128)(2,1)}) %all-gather.41.cloned.1.call-update) | async-done | bytes 1245200 | tf_op jit(solution)/shard_map/all_gather | solution.py:277
  765.2 4.0 fusion.96
  769.2 4.3 multiply_reduce_fusion
  781.0 4.9 convolution_convert_fusion.1
  793.4 13.8 %reduce-scatter.29.cloned.1.call-done = bf16[152,1,1024]{2,0,1:T(8,128)(2,1)} async-done(((bf16[608,1,1024]{2,0,1:T(8,128)(2,1)}), bf16[152,1,1024]{2,0,1:T(8,128)(2,1)}) %reduce-scatter.29.cloned.1.call-update) | async-done | bytes 311312 | tf_op jit(solution)/shard_map/reduce_scatter | solution.py:294
  809.5 5.8 pad_maximum_fusion.1
  815.3 8.7 copy.121
  825.3 4.7 convolution_convert_fusion.3
  842.1 8.7 copy.119
  853.5 80.5 %all-reduce.2.cloned.1.call-done = f32[2,12,1024]{2,0,1:T(2,128)} async-done(((f32[2,12,1024]{2,0,1:T(2,128)}), f32[2,12,1024]{2,0,1:T(2,128)}) %all-reduce.2.cloned.1.call-update) | async-done | bytes 98320 | tf_op jit(solution)/shard_map/psum | solution.py:356
  936.7 119.5 %reduce-scatter.33.cloned.1.call-done = bf16[128,3072]{1,0:T(8,128)(2,1)} async-done(((bf16[1024,3072]{1,0:T(8,128)(2,1)}), bf16[128,3072]{1,0:T(8,128)(2,1)}) %reduce-scatter.33.cloned.1.call-update) | async-done | bytes 786448
  1059.7 117.3 %reduce-scatter.31.cloned.1.call-done = bf16[128,3072]{1,0:T(8,128)(2,1)} async-done(((bf16[1024,3072]{1,0:T(8,128)(2,1)}), bf16[128,3072]{1,0:T(8,128)(2,1)}) %reduce-scatter.31.cloned.1.call-update) | async-done | bytes 786448
  (359 shorter events, 137.7 us)
Async XLA Ops:
  7.2 50.7 %copy-start.58 = (s32[608,1]{0,1:T(1,128)S(1)}, s32[608,1]{0,1:T(1,128)}, u32[]{:S(2)}) copy-start(s32[608,1]{0,1:T(1,128)} %param.33) | copy-start | bytes 7300
  7.2 50.8 %copy-start.37 = (bf16[2,256,128]{2,1,0:T(8,128)(2,1)S(1)}, bf16[2,256,128]{2,1,0:T(8,128)(2,1)}, u32[]{:S(2)}) copy-start(bf16[2,256,128]{2,1,0:T(8,128)(2,1)} %param.23) | copy-start | bytes 393220
  7.2 78.9 %all-gather.27.cloned.1.call-start = ((), (), s32[]{:S(2)}) async-start(), calls=%async_computation.10 | async-start | bytes 1556480 | tf_op jit(solution)/shard_map/all_gather | solution.py:171
  9.6 48.2 %copy-start.40 = (f32[152]{0:T(256)}, f32[152]{0:T(256)S(1)}, u32[]{:S(2)}) copy-start(f32[152]{0:T(256)S(1)} %add_rsqrt_fusion.3) | copy-start | bytes 1828
  39.3 63.6 %all-gather.43.cloned.1.call-start = ((), (), s32[]{:S(2)}) async-start(), calls=%async_computation.27 | async-start | bytes 1769472 | tf_op jit(solution)/shard_map/all_gather | solution.py:147
  41.2 97.4 %reduce-scatter.15.cloned.1.call-start = ((), (), s32[]{:S(2)}) async-start(), calls=%async_computation.11 | async-start | bytes 1556480 | tf_op jit(solution)/shard_map/reduce_scatter | solution.py:179
  86.1 25.8 %copy-start.10 = (bf16[1,256,1024]{2,1,0:T(8,128)(2,1)}, bf16[1,256,1024]{2,1,0:T(8,128)(2,1)S(1)}, u32[]{:S(2)}) copy-start(bf16[1,256,1024]{2,1,0:T(8,128)(2,1)S(1)} %all-gather.2) | copy-start | bytes 1572868
  111.9 27.8 %copy-start.17 = (bf16[4,64,608]{2,1,0:T(8,128)(2,1)}, bf16[4,64,608]{2,1,0:T(8,128)(2,1)S(1)}, u32[]{:S(2)}) copy-start(bf16[4,64,608]{2,1,0:T(8,128)(2,1)S(1)} %fusion.103) | copy-start | bytes 933892
  111.9 26.7 %copy-start.2 = (bf16[152,1,1024]{2,0,1:T(8,128)(2,1)S(1)}, bf16[152,1,1024]{2,0,1:T(8,128)(2,1)}, u32[]{:S(2)}) copy-start(bf16[152,1,1024]{2,0,1:T(8,128)(2,1)} %param.17) | copy-start | bytes 933892
  113.5 29.4 %copy-start.36 = (bf16[2,1024,128]{2,1,0:T(8,128)(2,1)S(1)}, bf16[2,1024,128]{2,1,0:T(8,128)(2,1)}, u32[]{:S(2)}) copy-start(bf16[2,1024,128]{2,1,0:T(8,128)(2,1)} %param.29) | copy-start | bytes 1572868
  113.5 30.3 %copy-start.57 = (bf16[2,512]{1,0:T(2,128)(2,1)S(1)}, bf16[2,512]{1,0:T(2,128)(2,1)}, u32[]{:S(2)}) copy-start(bf16[2,512]{1,0:T(2,128)(2,1)} %param.28) | copy-start | bytes 6148
  113.5 77.2 %all-gather.45.cloned.1.call-start = ((), (), s32[]{:S(2)}) async-start(), calls=%async_computation.28 | async-start | bytes 2359296 | tf_op jit(solution)/shard_map/all_gather | solution.py:148
  114.4 94.7 %all-gather.29.cloned.1.call-start = ((), (), s32[]{:S(2)}) async-start(), calls=%async_computation.12 | async-start | bytes 1556480 | tf_op jit(solution)/shard_map/all_gather | solution.py:193
  139.7 74.3 %copy-start.38 = (f32[152]{0:T(256)}, f32[152]{0:T(256)S(1)}, u32[]{:S(2)}) copy-start(f32[152]{0:T(256)S(1)} %broadcast_multiply_fusion.10) | copy-start | bytes 1828
  140.9 73.0 %copy-start.54 = (f32[152]{0:T(256)}, f32[152]{0:T(256)S(1)}, u32[]{:S(2)}) copy-start(f32[152]{0:T(256)S(1)} %add_rsqrt_fusion.2) | copy-start | bytes 1828
  142.9 120.0 %all-gather.47.cloned.1.call-start = ((), (), s32[]{:S(2)}) async-start(), calls=%async_computation.29 | async-start | bytes 2359296 | tf_op jit(solution)/shard_map/all_gather | solution.py:150
  143.8 148.5 %reduce-scatter.17.cloned.1.call-start = ((), (), s32[]{:S(2)}) async-start(), calls=%async_computation.13 | async-start | bytes 1556480 | tf_op jit(solution)/shard_map/reduce_scatter | solution.py:217
  170.0 92.9 %copy-start.59 = (f32[1,1024]{1,0:T(1,128)}, f32[1,1024]{1,0:T(1,128)S(1)}, u32[]{:S(2)}) copy-start(f32[1,1024]{1,0:T(1,128)S(1)} %fusion.162) | copy-start | bytes 12292
  262.9 29.4 %copy-start.3 = (bf16[152,1,1024]{2,0,1:T(8,128)(2,1)S(1)}, bf16[152,1,1024]{2,0,1:T(8,128)(2,1)}, u32[]{:S(2)}) copy-start(bf16[152,1,1024]{2,0,1:T(8,128)(2,1)} %reduce-scatter.15.cloned.1.call-done) | copy-start | bytes 933892
  267.8 73.3 %all-gather.49.cloned.1.call-start = ((), (), s32[]{:S(2)}) async-start(), calls=%async_computation.30 | async-start | bytes 1769472 | tf_op jit(solution)/shard_map/all_gather | solution.py:147
  268.6 91.4 %all-gather.31.cloned.1.call-start = ((), (), s32[]{:S(2)}) async-start(), calls=%async_computation.14 | async-start | bytes 1556480 | tf_op jit(solution)/shard_map/all_gather | solution.py:171
  293.7 70.1 %copy-start.51 = (f32[152]{0:T(256)}, f32[152]{0:T(256)S(1)}, u32[]{:S(2)}) copy-start(f32[152]{0:T(256)S(1)} %add_rsqrt_fusion.1) | copy-start | bytes 1828
  294.7 107.4 %reduce-scatter.19.cloned.1.call-start = ((), (), s32[]{:S(2)}) async-start(), calls=%async_computation.15 | async-start | bytes 1556480 | tf_op jit(solution)/shard_map/reduce_scatter | solution.py:179
  324.2 49.1 %copy-start.12 = (bf16[1,256,1024]{2,1,0:T(8,128)(2,1)}, bf16[1,256,1024]{2,1,0:T(8,128)(2,1)S(1)}, u32[]{:S(2)}) copy-start(bf16[1,256,1024]{2,1,0:T(8,128)(2,1)S(1)} %all-gather.8) | copy-start | bytes 1572868
  375.7 29.4 %copy-start.33 = (bf16[152,1,1024]{2,0,1:T(8,128)(2,1)S(1)}, bf16[152,1,1024]{2,0,1:T(8,128)(2,1)}, u32[]{:S(2)}) copy-start(bf16[152,1,1024]{2,0,1:T(8,128)(2,1)} %param.31) | copy-start | bytes 933892
  375.8 78.6 %all-gather.51.cloned.1.call-start = ((), (), s32[]{:S(2)}) async-start(), calls=%async_computation.31 | async-start | bytes 2359296 | tf_op jit(solution)/shard_map/all_gather | solution.py:148
  376.5 96.3 %all-gather.33.cloned.1.call-start = ((), (), s32[]{:S(2)}) async-start(), calls=%async_computation.16 | async-start | bytes 1556480 | tf_op jit(solution)/shard_map/all_gather | solution.py:193
  403.4 176.4 %copy-start.53 = (f32[152]{0:T(256)}, f32[152]{0:T(256)S(1)}, u32[]{:S(2)}) copy-start(f32[152]{0:T(256)S(1)} %add_rsqrt_fusion) | copy-start | bytes 1828
  404.3 88.5 %all-gather.35.cloned.1.call-start = ((), (), s32[]{:S(2)}) async-start(), calls=%async_computation.18 | async-start | bytes 1556480 | tf_op jit(solution)/shard_map/all_gather | solution.py:251
  406.0 140.0 %all-gather.53.cloned.1.call-start = ((), (), s32[]{:S(2)}) async-start(), calls=%async_computation.32 | async-start | bytes 2359296 | tf_op jit(solution)/shard_map/all_gather | solution.py:150
  406.6 173.2 %reduce-scatter.23.cloned.1.call-start = ((), (), s32[]{:S(2)}) async-start(), calls=%async_computation.19 | async-start | bytes 1556480 | tf_op jit(solution)/shard_map/reduce_scatter | solution.py:264
  432.8 122.5 %copy-start.63 = (f32[1,1024]{1,0:T(1,128)}, f32[1,1024]{1,0:T(1,128)S(1)}, u32[]{:S(2)}) copy-start(f32[1,1024]{1,0:T(1,128)S(1)} %fusion.161) | copy-start | bytes 12292
  555.3 53.0 %reduce-scatter.21.cloned.1.call-start = ((), (), s32[]{:S(2)}) async-start(), calls=%async_computation.17 | async-start | bytes 1556480 | tf_op jit(solution)/shard_map/reduce_scatter | solution.py:217
  560.3 69.7 %all-gather.37.cloned.1.call-start = ((), (), s32[]{:S(2)}) async-start(), calls=%async_computation.20 | async-start | bytes 1556480 | tf_op jit(solution)/shard_map/all_gather | solution.py:277
  612.0 71.0 %reduce-scatter.25.cloned.1.call-start = ((), (), s32[]{:S(2)}) async-start(), calls=%async_computation.21 | async-start | bytes 1556480 | tf_op jit(solution)/shard_map/reduce_scatter | solution.py:294
  652.8 30.2 %copy-start.52 = (f32[152]{0:T(256)S(1)}, f32[152]{0:T(256)}, u32[]{:S(2)}) copy-start(f32[152]{0:T(256)} %copy-done.51) | copy-start | bytes 1828
  656.7 48.3 %copy-start.60 = (f32[1,1024]{1,0:T(1,128)S(1)}, f32[1,1024]{1,0:T(1,128)}, u32[]{:S(2)}) copy-start(f32[1,1024]{1,0:T(1,128)} %copy-done.59) | copy-start | bytes 12292
  656.7 48.3 %all-gather.39.cloned.1.call-start = ((), (), s32[]{:S(2)}) async-start(), calls=%async_computation.22 | async-start | bytes 1556480 | tf_op jit(solution)/shard_map/all_gather | solution.py:251
  687.0 53.5 %reduce-scatter.27.cloned.1.call-start = ((), (), s32[]{:S(2)}) async-start(), calls=%async_computation.23 | async-start | bytes 1556480 | tf_op jit(solution)/shard_map/reduce_scatter | solution.py:264
  711.6 28.8 %copy-start.39 = (f32[152]{0:T(256)S(1)}, f32[152]{0:T(256)}, u32[]{:S(2)}) copy-start(f32[152]{0:T(256)} %copy-done.38) | copy-start | bytes 1828
  711.6 28.8 %copy-start.55 = (f32[152]{0:T(256)S(1)}, f32[152]{0:T(256)}, u32[]{:S(2)}) copy-start(f32[152]{0:T(256)} %copy-done.54) | copy-start | bytes 1828
  714.2 31.0 %copy-start.64 = (f32[1,1024]{1,0:T(1,128)S(1)}, f32[1,1024]{1,0:T(1,128)}, u32[]{:S(2)}) copy-start(f32[1,1024]{1,0:T(1,128)} %copy-done.63) | copy-start | bytes 12292
  714.2 48.9 %all-gather.41.cloned.1.call-start = ((), (), s32[]{:S(2)}) async-start(), calls=%async_computation.24 | async-start | bytes 1556480 | tf_op jit(solution)/shard_map/all_gather | solution.py:277
  745.2 62.0 %reduce-scatter.29.cloned.1.call-start = ((), (), s32[]{:S(2)}) async-start(), calls=%async_computation.25 | async-start | bytes 1556480 | tf_op jit(solution)/shard_map/reduce_scatter | solution.py:294
  780.9 153.0 %all-reduce.2.cloned.1.call-start = ((), (), s32[]{:S(2)}) async-start(), calls=%async_computation.26 | async-start | bytes 196608 | tf_op jit(solution)/shard_map/psum | solution.py:356
  790.3 18.3 %copy-start.48 = (f32[1024]{0:T(1024)S(1)}, f32[1024]{0:T(1024)}, u32[]{:S(2)}) copy-start(f32[1024]{0:T(1024)} %get-tuple-element.134) | copy-start | bytes 12292
  809.5 246.7 %reduce-scatter.33.cloned.1.call-start = ((), (), s32[]{:S(2)}) async-start(), calls=%async_computation.34 | async-start | bytes 7077888
  824.0 352.9 %reduce-scatter.31.cloned.1.call-start = ((), (), s32[]{:S(2)}) async-start(), calls=%async_computation.33 | async-start | bytes 7077888
  (55 other events, 243.1 us)
Sparse Core Ops, SparseCore 0:
  39.4 15.0 all-gather.26
  57.3 45.6 all-gather.42
  113.6 24.8 reduce-scatter.14
  141.3 49.3 all-gather.44
  192.8 16.2 all-gather.28
  211.8 51.0 all-gather.46
  267.9 24.2 reduce-scatter.16
  295.0 46.0 all-gather.48
  343.3 16.6 all-gather.30
  375.9 26.1 reduce-scatter.18
  405.0 49.3 all-gather.50
  456.4 16.2 all-gather.32
  475.0 17.8 all-gather.34
  494.9 51.0 all-gather.52
  555.4 24.2 reduce-scatter.22
  582.2 26.1 reduce-scatter.20
  612.1 17.8 all-gather.36
  656.8 26.1 reduce-scatter.24
  687.1 17.7 all-gather.38
  714.4 26.0 reduce-scatter.26
  745.3 17.8 all-gather.40
  781.0 26.1 reduce-scatter.28
  813.4 120.5 all-reduce.1
  937.4 118.7 reduce-scatter.32
  1059.8 117.0 reduce-scatter.30
